TPU v7x, 256 devices: a whole 4x4x8 slice. The times are simulated.
256 devices in a mesh: lvl: 4 (over x), gx: 16 (over z_hi, y), gy: 4 (over z_lo, core).
Axes of the slice: x: 4, y: 4, z: 8 (z_hi: 4, z_lo: 2; z = z_hi * 2 + z_lo), core: 2. Of those that a mesh axis runs over, the one named last changes fastest.
Arguments:
- initial: float32 [16, 128, 32, 128], P(None, 'gx', 'gy'), may hold values from 0.07 to 1, as said below
- rate_factor: float32 [128, 32, 128], P('gx', 'gy'), may hold values from 0.5 to 2
- diffusivity: float32 [16], replicated, may hold values from 0.3 to 2
- loss_rate: float32 [16], replicated, may hold values from 0.05 to 1.5
- quench: float32 [16, 16], replicated, may hold values from 0 to 0.1
- formation: float32 [16, 16], replicated, may hold values from 0 to 0.1
Outputs:
- final: float32 [4, 16, 128, 32, 128], P('lvl', None, 'gx', 'gy')
Inputs may be any that keep to these rules, and one draw needn't show every extreme that they name: `initial`: positive concentrations.
All inputs are finite; a program needn't handle non-finite values.
Results may differ from a plain program's by a relative error of at most 0.0001.
Values sent between devices are 32-bit elements; how exact they have to be, the bound alone decides.
A program may use at most 64 MiB of HBM per device.

v0:
```python
import jax
import jax.numpy as jnp
from jax import lax
from jax.sharding import PartitionSpec as P

REACT = 11
STEPS = 4
SWEEPS = 4


def padded_2(x, sides, width):
    for axis, dim in sides:
        size, length = (lax.axis_size(axis), x.shape[dim])
        up = [(i, (i + 1) % size) for i in range(size - 1)]
        down = [(j, i) for i, j in up]
        last = lax.slice_in_dim(x, length - width, length, axis=dim)
        leading = lax.slice_in_dim(x, 0, width, axis=dim)
        before = lax.ppermute(last, axis, up)
        after = lax.ppermute(leading, axis, down)
        x = jnp.concatenate([before, x, after], axis=dim)
    return x


def from_behind(value, axis, steps):
    count = lax.axis_size(axis)
    leading, last = (max(0, -steps), min(count, count - steps))
    return lax.ppermute(value, axis, [(source, source + steps) for source in range(leading, last)])


def conduct(fields, diffusivity):
    return diffusivity[:, None, None, None] * (1.0 + fields * fields)


def face_weights(padded, diffusivity):
    conductance = conduct(padded, diffusivity)
    centre = conductance[:, 1:-1, 1:-1]
    inner_cells = padded[:, 1:-1, 1:-1]
    vertical = conduct(jnp.pad(inner_cells, ((0, 0), (0, 0), (0, 0), (1, 1))), diffusivity)
    west_face = 0.5 * (centre + conductance[:, :-2, 1:-1])
    east_face = 0.5 * (centre + conductance[:, 2:, 1:-1])
    south_face = 0.5 * (centre + conductance[:, 1:-1, :-2])
    north_face = 0.5 * (centre + conductance[:, 1:-1, 2:])
    lower_face = 0.5 * (centre + vertical[..., :-2])
    upper_face = 0.5 * (centre + vertical[..., 2:])
    weight_sum = west_face + east_face + south_face + north_face + lower_face + upper_face
    return ((west_face, east_face, south_face, north_face, lower_face, upper_face), weight_sum)


def neighbours(padded, coeffs):
    west_face, east_face, south_face, north_face, lower_face, upper_face = coeffs
    inner_cells = padded[:, 1:-1, 1:-1]
    stacked = jnp.pad(inner_cells, ((0, 0), (0, 0), (0, 0), (1, 1)))
    return (
        west_face * padded[:, :-2, 1:-1]
        + east_face * padded[:, 2:, 1:-1]
        + south_face * padded[:, 1:-1, :-2]
        + north_face * padded[:, 1:-1, 2:]
        + lower_face * stacked[..., :-2]
        + upper_face * stacked[..., 2:]
    )


def chemistry(fields, rate_factor, loss_rate, quench, formation):
    reacting = (jnp.arange(fields.shape[0]) < REACT).astype(jnp.float32)[:, None, None, None]
    squares = jnp.einsum("ij,jxyz->ixyz", quench, fields * fields, precision=lax.Precision.HIGHEST)
    produced = jnp.einsum("ij,jxyz->ixyz", formation, fields, precision=lax.Precision.HIGHEST)
    loss_term = reacting * loss_rate[:, None, None, None] * rate_factor[None] * (1.0 + squares)
    production = reacting * rate_factor[None] * produced
    return (loss_term, production)


def on_device(initial, rate_factor, diffusivity, loss_rate, quench, formation):
    level_index = lax.axis_index("lvl")
    current_state = initial
    carried = jnp.zeros_like(initial)
    received_prev = jnp.zeros_like(initial)
    for tick_index in range(STEPS + lax.axis_size("lvl") - 1):
        node_index = tick_index - level_index
        advance = (node_index >= 0) & (node_index < STEPS)
        padded = padded_2(current_state, (("gx", 1), ("gy", 2)), 1)
        coeffs, weight_sum = face_weights(padded, diffusivity)
        loss_term, production = chemistry(current_state, rate_factor, loss_rate, quench, formation)
        diffused = neighbours(padded, coeffs) - weight_sum * current_state
        tendency = diffused + production - loss_term * current_state
        received_tendency, received_carried = from_behind((tendency, carried), "lvl", 1)
        inflow = 0.5 * (received_prev + received_tendency) - received_carried
        received_prev = received_tendency
        right_side = current_state + production + inflow
        denominator = 1.0 + loss_term + weight_sum
        iterate = current_state
        padded_now = padded
        for sweep_index in range(SWEEPS):
            if sweep_index > 0:
                padded_now = padded_2(iterate, (("gx", 1), ("gy", 2)), 1)
            iterate = (right_side + neighbours(padded_now, coeffs)) / denominator
        carried = production + (iterate - right_side)
        current_state = jnp.where(advance, iterate, current_state)
    return current_state[None]


def solution(mesh):
    in_specs = (P(None, "gx", "gy", None), P("gx", "gy", None), P(), P(), P(), P())
    out_specs = P("lvl", None, "gx", "gy", None)
    return jax.shard_map(
        on_device, mesh=mesh, in_specs=in_specs, out_specs=out_specs, check_vma=False
    )
```

profile of v0, /device:TPU:91, one launch (start us, length us, event | category | flops | bytes accessed | tf_op | source)
XLA Modules:
  0.0 773.1 jit_solution(4354906624033468198)
XLA Ops:
  32.1 10.3 %collective-permute-done.4 = f32[16,8,8,128]{3,0,2,1:T(8,128)S(1)} collective-permute-done((f32[16,8,8,128]{3,0,2,1:T(8,128)S(1)}, f32[16,8,8,128]{3,0,2,1:T(8,128)S(1)}, u32[]{:S(2)}, u32[]{:S(2)}) %collective-permute-start.4) | collective-permute-done | bytes 524320 | tf_op jit(solution)/shard_map/ppermute | solution.py:27
  49.5 8.0 %collective-permute-done.7 = f32[16,1,8,128]{3,0,2,1:T(8,128)S(1)} collective-permute-done((f32[16,1,8,128]{3,0,2,1:T(8,128)S(1)}, f32[16,1,8,128]{3,0,2,1:T(8,128)S(1)}, u32[]{:S(2)}, u32[]{:S(2)}) %collective-permute-start.7) | collective-permute-done | bytes 65568 | tf_op jit(solution)/shard_map/ppermute | solution.py:19
  71.8 6.6 collective-permute-done.11
  92.5 6.6 collective-permute-done.15
  116.9 6.0 collective-permute-done.19
  135.2 8.2 %collective-permute-done.23 = f32[16,8,8,128]{3,0,2,1:T(8,128)S(1)} collective-permute-done((f32[16,8,8,128]{3,0,2,1:T(8,128)S(1)}, f32[16,8,8,128]{3,0,2,1:T(8,128)S(1)}, u32[]{:S(2)}, u32[]{:S(2)}) %collective-permute-start.23) | collective-permute-done | bytes 524320 | tf_op jit(solution)/shard_map/ppermute | solution.py:27
  143.4 10.9 %collective-permute-done.22 = f32[16,8,8,128]{3,0,2,1:T(8,128)S(1)} collective-permute-done((f32[16,8,8,128]{3,0,2,1:T(8,128)S(1)}, f32[16,8,8,128]{3,0,2,1:T(8,128)S(1)}, u32[]{:S(2)}, u32[]{:S(2)}) %collective-permute-start.22) | collective-permute-done | bytes 524320 | tf_op jit(solution)/shard_map/ppermute | solution.py:27
  181.9 6.6 collective-permute-done.29
  202.5 6.6 collective-permute-done.33
  227.0 6.0 collective-permute-done.37
  245.2 8.3 %collective-permute-done.41 = f32[16,8,8,128]{3,0,2,1:T(8,128)S(1)} collective-permute-done((f32[16,8,8,128]{3,0,2,1:T(8,128)S(1)}, f32[16,8,8,128]{3,0,2,1:T(8,128)S(1)}, u32[]{:S(2)}, u32[]{:S(2)}) %collective-permute-start.41) | collective-permute-done | bytes 524320 | tf_op jit(solution)/shard_map/ppermute | solution.py:27
  253.5 10.9 %collective-permute-done.40 = f32[16,8,8,128]{3,0,2,1:T(8,128)S(1)} collective-permute-done((f32[16,8,8,128]{3,0,2,1:T(8,128)S(1)}, f32[16,8,8,128]{3,0,2,1:T(8,128)S(1)}, u32[]{:S(2)}, u32[]{:S(2)}) %collective-permute-start.40) | collective-permute-done | bytes 524320 | tf_op jit(solution)/shard_map/ppermute | solution.py:27
  291.9 6.6 collective-permute-done.47
  312.5 6.6 collective-permute-done.51
  336.5 6.0 collective-permute-done.55
  354.9 8.1 %collective-permute-done.59 = f32[16,8,8,128]{3,0,2,1:T(8,128)S(1)} collective-permute-done((f32[16,8,8,128]{3,0,2,1:T(8,128)S(1)}, f32[16,8,8,128]{3,0,2,1:T(8,128)S(1)}, u32[]{:S(2)}, u32[]{:S(2)}) %collective-permute-start.59) | collective-permute-done | bytes 524320 | tf_op jit(solution)/shard_map/ppermute | solution.py:27
  363.0 10.9 %collective-permute-done.58 = f32[16,8,8,128]{3,0,2,1:T(8,128)S(1)} collective-permute-done((f32[16,8,8,128]{3,0,2,1:T(8,128)S(1)}, f32[16,8,8,128]{3,0,2,1:T(8,128)S(1)}, u32[]{:S(2)}, u32[]{:S(2)}) %collective-permute-start.58) | collective-permute-done | bytes 524320 | tf_op jit(solution)/shard_map/ppermute | solution.py:27
  422.6 6.6 collective-permute-done.69
  447.0 6.0 collective-permute-done.73
  465.2 8.3 %collective-permute-done.77 = f32[16,8,8,128]{3,0,2,1:T(8,128)S(1)} collective-permute-done((f32[16,8,8,128]{3,0,2,1:T(8,128)S(1)}, f32[16,8,8,128]{3,0,2,1:T(8,128)S(1)}, u32[]{:S(2)}, u32[]{:S(2)}) %collective-permute-start.77) | collective-permute-done | bytes 524320 | tf_op jit(solution)/shard_map/ppermute | solution.py:27
  473.5 10.9 %collective-permute-done.76 = f32[16,8,8,128]{3,0,2,1:T(8,128)S(1)} collective-permute-done((f32[16,8,8,128]{3,0,2,1:T(8,128)S(1)}, f32[16,8,8,128]{3,0,2,1:T(8,128)S(1)}, u32[]{:S(2)}, u32[]{:S(2)}) %collective-permute-start.76) | collective-permute-done | bytes 524320 | tf_op jit(solution)/shard_map/ppermute | solution.py:27
  512.1 6.6 collective-permute-done.83
  533.1 6.2 collective-permute-done.87
  575.9 8.2 %collective-permute-done.95 = f32[16,8,8,128]{3,0,2,1:T(8,128)S(1)} collective-permute-done((f32[16,8,8,128]{3,0,2,1:T(8,128)S(1)}, f32[16,8,8,128]{3,0,2,1:T(8,128)S(1)}, u32[]{:S(2)}, u32[]{:S(2)}) %collective-permute-start.95) | collective-permute-done | bytes 524320 | tf_op jit(solution)/shard_map/ppermute | solution.py:27
  584.1 10.9 %collective-permute-done.94 = f32[16,8,8,128]{3,0,2,1:T(8,128)S(1)} collective-permute-done((f32[16,8,8,128]{3,0,2,1:T(8,128)S(1)}, f32[16,8,8,128]{3,0,2,1:T(8,128)S(1)}, u32[]{:S(2)}, u32[]{:S(2)}) %collective-permute-start.94) | collective-permute-done | bytes 524320 | tf_op jit(solution)/shard_map/ppermute | solution.py:27
  622.8 6.6 collective-permute-done.101
  643.8 6.6 collective-permute-done.105
  668.2 6.0 collective-permute-done.109
  686.4 8.3 %collective-permute-done.113 = f32[16,8,8,128]{3,0,2,1:T(8,128)S(1)} collective-permute-done((f32[16,8,8,128]{3,0,2,1:T(8,128)S(1)}, f32[16,8,8,128]{3,0,2,1:T(8,128)S(1)}, u32[]{:S(2)}, u32[]{:S(2)}) %collective-permute-start.113) | collective-permute-done | bytes 524320 | tf_op jit(solution)/shard_map/ppermute | solution.py:27
  694.7 10.9 %collective-permute-done.112 = f32[16,8,8,128]{3,0,2,1:T(8,128)S(1)} collective-permute-done((f32[16,8,8,128]{3,0,2,1:T(8,128)S(1)}, f32[16,8,8,128]{3,0,2,1:T(8,128)S(1)}, u32[]{:S(2)}, u32[]{:S(2)}) %collective-permute-start.112) | collective-permute-done | bytes 524320 | tf_op jit(solution)/shard_map/ppermute | solution.py:27
  733.1 6.6 collective-permute-done.119
  754.1 6.6 collective-permute-done.123
  (463 shorter events, 522.2 us)
Async XLA Ops:
  1.4 12.3 %collective-permute-start = (f32[16,1,8,128]{3,0,2,1:T(8,128)S(1)}, f32[16,1,8,128]{3,0,2,1:T(8,128)S(1)}, u32[]{:S(2)}, u32[]{:S(2)}) collective-permute-start(f32[16,1,8,128]{3,0,2,1:T(8,128)S(1)} %get-tuple-element.198), channel_id=1, source_target_pairs={{0,4},{4,8},{8,12},{12,16},{16,20},{20,24},{24,28},{28,32},{32,36}... | collective-permute-start | bytes 196616 | tf_op jit(solution)/shard_map/ppermute | solution.py:18
  9.3 22.8 %collective-permute-start.5 = (f32[16,8,8,128]{3,0,2,1:T(8,128)S(1)}, f32[16,8,8,128]{3,0,2,1:T(8,128)S(1)}, u32[]{:S(2)}, u32[]{:S(2)}) collective-permute-start(f32[16,8,8,128]{3,0,2,1:T(8,128)S(1)} %broadcast_in_dim.4), channel_id=1, source_target_pairs={{0,64},{64,128},{128,192},{1,65},{65,129},{129,193},{2,66},{66,130... | collective-permute-start | bytes 1572872 | tf_op jit(solution)/shard_map/ppermute | solution.py:27
  28.9 13.4 %collective-permute-start.4 = (f32[16,8,8,128]{3,0,2,1:T(8,128)S(1)}, f32[16,8,8,128]{3,0,2,1:T(8,128)S(1)}, u32[]{:S(2)}, u32[]{:S(2)}) collective-permute-start(f32[16,8,8,128]{3,0,2,1:T(8,128)S(1)} %get-tuple-element.79), channel_id=1, source_target_pairs={{0,64},{64,128},{128,192},{1,65},{65,129},{129,193},{2,66},{66,130... | collective-permute-start | bytes 1572872 | tf_op jit(solution)/shard_map/ppermute | solution.py:27
  47.6 9.9 %collective-permute-start.7 = (f32[16,1,8,128]{3,0,2,1:T(8,128)S(1)}, f32[16,1,8,128]{3,0,2,1:T(8,128)S(1)}, u32[]{:S(2)}, u32[]{:S(2)}) collective-permute-start(f32[16,1,8,128]{3,0,2,1:T(8,128)S(1)} %get-tuple-element.196), channel_id=1, source_target_pairs={{4,0},{8,4},{12,8},{16,12},{20,16},{24,20},{28,24},{32,28},{36,32}... | collective-permute-start | bytes 196616 | tf_op jit(solution)/shard_map/ppermute | solution.py:19
  68.4 10.0 %collective-permute-start.11 = (f32[16,1,8,128]{3,0,2,1:T(8,128)S(1)}, f32[16,1,8,128]{3,0,2,1:T(8,128)S(1)}, u32[]{:S(2)}, u32[]{:S(2)}) collective-permute-start(f32[16,1,8,128]{3,0,2,1:T(8,128)S(1)} %get-tuple-element.194), channel_id=1, source_target_pairs={{4,0},{8,4},{12,8},{16,12},{20,16},{24,20},{28,24},{32,28},{36,32}... | collective-permute-start | bytes 196616 | tf_op jit(solution)/shard_map/ppermute | solution.py:19
  89.1 9.9 %collective-permute-start.15 = (f32[16,1,8,128]{3,0,2,1:T(8,128)S(1)}, f32[16,1,8,128]{3,0,2,1:T(8,128)S(1)}, u32[]{:S(2)}, u32[]{:S(2)}) collective-permute-start(f32[16,1,8,128]{3,0,2,1:T(8,128)S(1)} %get-tuple-element.192), channel_id=1, source_target_pairs={{4,0},{8,4},{12,8},{16,12},{20,16},{24,20},{28,24},{32,28},{36,32}... | collective-permute-start | bytes 196616 | tf_op jit(solution)/shard_map/ppermute | solution.py:19
  112.9 9.9 %collective-permute-start.19 = (f32[16,1,8,128]{3,0,2,1:T(8,128)S(1)}, f32[16,1,8,128]{3,0,2,1:T(8,128)S(1)}, u32[]{:S(2)}, u32[]{:S(2)}) collective-permute-start(f32[16,1,8,128]{3,0,2,1:T(8,128)S(1)} %get-tuple-element.190), channel_id=1, source_target_pairs={{4,0},{8,4},{12,8},{16,12},{20,16},{24,20},{28,24},{32,28},{36,32}... | collective-permute-start | bytes 196616 | tf_op jit(solution)/shard_map/ppermute | solution.py:19
  127.6 15.8 %collective-permute-start.23 = (f32[16,8,8,128]{3,0,2,1:T(8,128)S(1)}, f32[16,8,8,128]{3,0,2,1:T(8,128)S(1)}, u32[]{:S(2)}, u32[]{:S(2)}) collective-permute-start(f32[16,8,8,128]{3,0,2,1:T(8,128)S(1)} %subtract_add_fusion.11), channel_id=1, source_target_pairs={{0,64},{64,128},{128,192},{1,65},{65,129},{129,193},{2,66},{66,130... | collective-permute-start | bytes 1572872 | tf_op jit(solution)/shard_map/ppermute | solution.py:27
  132.3 22.0 %collective-permute-start.22 = (f32[16,8,8,128]{3,0,2,1:T(8,128)S(1)}, f32[16,8,8,128]{3,0,2,1:T(8,128)S(1)}, u32[]{:S(2)}, u32[]{:S(2)}) collective-permute-start(f32[16,8,8,128]{3,0,2,1:T(8,128)S(1)} %get-tuple-element.67), channel_id=1, source_target_pairs={{0,64},{64,128},{128,192},{1,65},{65,129},{129,193},{2,66},{66,130... | collective-permute-start | bytes 1572872 | tf_op jit(solution)/shard_map/ppermute | solution.py:27
  178.5 9.9 %collective-permute-start.29 = (f32[16,1,8,128]{3,0,2,1:T(8,128)S(1)}, f32[16,1,8,128]{3,0,2,1:T(8,128)S(1)}, u32[]{:S(2)}, u32[]{:S(2)}) collective-permute-start(f32[16,1,8,128]{3,0,2,1:T(8,128)S(1)} %get-tuple-element.186), channel_id=1, source_target_pairs={{4,0},{8,4},{12,8},{16,12},{20,16},{24,20},{28,24},{32,28},{36,32}... | collective-permute-start | bytes 196616 | tf_op jit(solution)/shard_map/ppermute | solution.py:19
  199.2 9.9 %collective-permute-start.33 = (f32[16,1,8,128]{3,0,2,1:T(8,128)S(1)}, f32[16,1,8,128]{3,0,2,1:T(8,128)S(1)}, u32[]{:S(2)}, u32[]{:S(2)}) collective-permute-start(f32[16,1,8,128]{3,0,2,1:T(8,128)S(1)} %get-tuple-element.184), channel_id=1, source_target_pairs={{4,0},{8,4},{12,8},{16,12},{20,16},{24,20},{28,24},{32,28},{36,32}... | collective-permute-start | bytes 196616 | tf_op jit(solution)/shard_map/ppermute | solution.py:19
  223.0 9.9 %collective-permute-start.37 = (f32[16,1,8,128]{3,0,2,1:T(8,128)S(1)}, f32[16,1,8,128]{3,0,2,1:T(8,128)S(1)}, u32[]{:S(2)}, u32[]{:S(2)}) collective-permute-start(f32[16,1,8,128]{3,0,2,1:T(8,128)S(1)} %get-tuple-element.182), channel_id=1, source_target_pairs={{4,0},{8,4},{12,8},{16,12},{20,16},{24,20},{28,24},{32,28},{36,32}... | collective-permute-start | bytes 196616 | tf_op jit(solution)/shard_map/ppermute | solution.py:19
  237.7 15.8 %collective-permute-start.41 = (f32[16,8,8,128]{3,0,2,1:T(8,128)S(1)}, f32[16,8,8,128]{3,0,2,1:T(8,128)S(1)}, u32[]{:S(2)}, u32[]{:S(2)}) collective-permute-start(f32[16,8,8,128]{3,0,2,1:T(8,128)S(1)} %get-tuple-element.63), channel_id=1, source_target_pairs={{0,64},{64,128},{128,192},{1,65},{65,129},{129,193},{2,66},{66,130... | collective-permute-start | bytes 1572872 | tf_op jit(solution)/shard_map/ppermute | solution.py:27
  242.3 22.1 %collective-permute-start.40 = (f32[16,8,8,128]{3,0,2,1:T(8,128)S(1)}, f32[16,8,8,128]{3,0,2,1:T(8,128)S(1)}, u32[]{:S(2)}, u32[]{:S(2)}) collective-permute-start(f32[16,8,8,128]{3,0,2,1:T(8,128)S(1)} %get-tuple-element.55), channel_id=1, source_target_pairs={{0,64},{64,128},{128,192},{1,65},{65,129},{129,193},{2,66},{66,130... | collective-permute-start | bytes 1572872 | tf_op jit(solution)/shard_map/ppermute | solution.py:27
  288.5 9.9 %collective-permute-start.47 = (f32[16,1,8,128]{3,0,2,1:T(8,128)S(1)}, f32[16,1,8,128]{3,0,2,1:T(8,128)S(1)}, u32[]{:S(2)}, u32[]{:S(2)}) collective-permute-start(f32[16,1,8,128]{3,0,2,1:T(8,128)S(1)} %get-tuple-element.178), channel_id=1, source_target_pairs={{4,0},{8,4},{12,8},{16,12},{20,16},{24,20},{28,24},{32,28},{36,32}... | collective-permute-start | bytes 196616 | tf_op jit(solution)/shard_map/ppermute | solution.py:19
  309.2 9.9 %collective-permute-start.51 = (f32[16,1,8,128]{3,0,2,1:T(8,128)S(1)}, f32[16,1,8,128]{3,0,2,1:T(8,128)S(1)}, u32[]{:S(2)}, u32[]{:S(2)}) collective-permute-start(f32[16,1,8,128]{3,0,2,1:T(8,128)S(1)} %get-tuple-element.176), channel_id=1, source_target_pairs={{4,0},{8,4},{12,8},{16,12},{20,16},{24,20},{28,24},{32,28},{36,32}... | collective-permute-start | bytes 196616 | tf_op jit(solution)/shard_map/ppermute | solution.py:19
  332.5 9.9 %collective-permute-start.55 = (f32[16,1,8,128]{3,0,2,1:T(8,128)S(1)}, f32[16,1,8,128]{3,0,2,1:T(8,128)S(1)}, u32[]{:S(2)}, u32[]{:S(2)}) collective-permute-start(f32[16,1,8,128]{3,0,2,1:T(8,128)S(1)} %get-tuple-element.174), channel_id=1, source_target_pairs={{4,0},{8,4},{12,8},{16,12},{20,16},{24,20},{28,24},{32,28},{36,32}... | collective-permute-start | bytes 196616 | tf_op jit(solution)/shard_map/ppermute | solution.py:19
  347.1 15.8 %collective-permute-start.59 = (f32[16,8,8,128]{3,0,2,1:T(8,128)S(1)}, f32[16,8,8,128]{3,0,2,1:T(8,128)S(1)}, u32[]{:S(2)}, u32[]{:S(2)}) collective-permute-start(f32[16,8,8,128]{3,0,2,1:T(8,128)S(1)} %subtract_add_fusion.7), channel_id=1, source_target_pairs={{0,64},{64,128},{128,192},{1,65},{65,129},{129,193},{2,66},{66,130... | collective-permute-start | bytes 1572872 | tf_op jit(solution)/shard_map/ppermute | solution.py:27
  351.9 22.0 %collective-permute-start.58 = (f32[16,8,8,128]{3,0,2,1:T(8,128)S(1)}, f32[16,8,8,128]{3,0,2,1:T(8,128)S(1)}, u32[]{:S(2)}, u32[]{:S(2)}) collective-permute-start(f32[16,8,8,128]{3,0,2,1:T(8,128)S(1)} %get-tuple-element.43), channel_id=1, source_target_pairs={{0,64},{64,128},{128,192},{1,65},{65,129},{129,193},{2,66},{66,130... | collective-permute-start | bytes 1572872 | tf_op jit(solution)/shard_map/ppermute | solution.py:27
  419.2 9.9 %collective-permute-start.69 = (f32[16,1,8,128]{3,0,2,1:T(8,128)S(1)}, f32[16,1,8,128]{3,0,2,1:T(8,128)S(1)}, u32[]{:S(2)}, u32[]{:S(2)}) collective-permute-start(f32[16,1,8,128]{3,0,2,1:T(8,128)S(1)} %get-tuple-element.168), channel_id=1, source_target_pairs={{4,0},{8,4},{12,8},{16,12},{20,16},{24,20},{28,24},{32,28},{36,32}... | collective-permute-start | bytes 196616 | tf_op jit(solution)/shard_map/ppermute | solution.py:19
  443.1 9.9 %collective-permute-start.73 = (f32[16,1,8,128]{3,0,2,1:T(8,128)S(1)}, f32[16,1,8,128]{3,0,2,1:T(8,128)S(1)}, u32[]{:S(2)}, u32[]{:S(2)}) collective-permute-start(f32[16,1,8,128]{3,0,2,1:T(8,128)S(1)} %get-tuple-element.166), channel_id=1, source_target_pairs={{4,0},{8,4},{12,8},{16,12},{20,16},{24,20},{28,24},{32,28},{36,32}... | collective-permute-start | bytes 196616 | tf_op jit(solution)/shard_map/ppermute | solution.py:19
  457.7 15.8 %collective-permute-start.77 = (f32[16,8,8,128]{3,0,2,1:T(8,128)S(1)}, f32[16,8,8,128]{3,0,2,1:T(8,128)S(1)}, u32[]{:S(2)}, u32[]{:S(2)}) collective-permute-start(f32[16,8,8,128]{3,0,2,1:T(8,128)S(1)} %get-tuple-element.39), channel_id=1, source_target_pairs={{0,64},{64,128},{128,192},{1,65},{65,129},{129,193},{2,66},{66,130... | collective-permute-start | bytes 1572872 | tf_op jit(solution)/shard_map/ppermute | solution.py:27
  462.4 22.1 %collective-permute-start.76 = (f32[16,8,8,128]{3,0,2,1:T(8,128)S(1)}, f32[16,8,8,128]{3,0,2,1:T(8,128)S(1)}, u32[]{:S(2)}, u32[]{:S(2)}) collective-permute-start(f32[16,8,8,128]{3,0,2,1:T(8,128)S(1)} %get-tuple-element.31), channel_id=1, source_target_pairs={{0,64},{64,128},{128,192},{1,65},{65,129},{129,193},{2,66},{66,130... | collective-permute-start | bytes 1572872 | tf_op jit(solution)/shard_map/ppermute | solution.py:27
  508.7 9.9 %collective-permute-start.83 = (f32[16,1,8,128]{3,0,2,1:T(8,128)S(1)}, f32[16,1,8,128]{3,0,2,1:T(8,128)S(1)}, u32[]{:S(2)}, u32[]{:S(2)}) collective-permute-start(f32[16,1,8,128]{3,0,2,1:T(8,128)S(1)} %get-tuple-element.162), channel_id=1, source_target_pairs={{4,0},{8,4},{12,8},{16,12},{20,16},{24,20},{28,24},{32,28},{36,32}... | collective-permute-start | bytes 196616 | tf_op jit(solution)/shard_map/ppermute | solution.py:19
  553.6 9.9 %collective-permute-start.91 = (f32[16,1,8,128]{3,0,2,1:T(8,128)S(1)}, f32[16,1,8,128]{3,0,2,1:T(8,128)S(1)}, u32[]{:S(2)}, u32[]{:S(2)}) collective-permute-start(f32[16,1,8,128]{3,0,2,1:T(8,128)S(1)} %get-tuple-element.158), channel_id=1, source_target_pairs={{4,0},{8,4},{12,8},{16,12},{20,16},{24,20},{28,24},{32,28},{36,32}... | collective-permute-start | bytes 196616 | tf_op jit(solution)/shard_map/ppermute | solution.py:19
  568.3 15.8 %collective-permute-start.95 = (f32[16,8,8,128]{3,0,2,1:T(8,128)S(1)}, f32[16,8,8,128]{3,0,2,1:T(8,128)S(1)}, u32[]{:S(2)}, u32[]{:S(2)}) collective-permute-start(f32[16,8,8,128]{3,0,2,1:T(8,128)S(1)} %subtract_add_fusion.3), channel_id=1, source_target_pairs={{0,64},{64,128},{128,192},{1,65},{65,129},{129,193},{2,66},{66,130... | collective-permute-start | bytes 1572872 | tf_op jit(solution)/shard_map/ppermute | solution.py:27
  573.0 22.0 %collective-permute-start.94 = (f32[16,8,8,128]{3,0,2,1:T(8,128)S(1)}, f32[16,8,8,128]{3,0,2,1:T(8,128)S(1)}, u32[]{:S(2)}, u32[]{:S(2)}) collective-permute-start(f32[16,8,8,128]{3,0,2,1:T(8,128)S(1)} %get-tuple-element.19), channel_id=1, source_target_pairs={{0,64},{64,128},{128,192},{1,65},{65,129},{129,193},{2,66},{66,130... | collective-permute-start | bytes 1572872 | tf_op jit(solution)/shard_map/ppermute | solution.py:27
  619.5 9.9 %collective-permute-start.101 = (f32[16,1,8,128]{3,0,2,1:T(8,128)S(1)}, f32[16,1,8,128]{3,0,2,1:T(8,128)S(1)}, u32[]{:S(2)}, u32[]{:S(2)}) collective-permute-start(f32[16,1,8,128]{3,0,2,1:T(8,128)S(1)} %get-tuple-element.154), channel_id=1, source_target_pairs={{4,0},{8,4},{12,8},{16,12},{20,16},{24,20},{28,24},{32,28},{36,32}... | collective-permute-start | bytes 196616 | tf_op jit(solution)/shard_map/ppermute | solution.py:19
  640.4 9.9 %collective-permute-start.105 = (f32[16,1,8,128]{3,0,2,1:T(8,128)S(1)}, f32[16,1,8,128]{3,0,2,1:T(8,128)S(1)}, u32[]{:S(2)}, u32[]{:S(2)}) collective-permute-start(f32[16,1,8,128]{3,0,2,1:T(8,128)S(1)} %get-tuple-element.152), channel_id=1, source_target_pairs={{4,0},{8,4},{12,8},{16,12},{20,16},{24,20},{28,24},{32,28},{36,32}... | collective-permute-start | bytes 196616 | tf_op jit(solution)/shard_map/ppermute | solution.py:19
  678.9 15.8 %collective-permute-start.113 = (f32[16,8,8,128]{3,0,2,1:T(8,128)S(1)}, f32[16,8,8,128]{3,0,2,1:T(8,128)S(1)}, u32[]{:S(2)}, u32[]{:S(2)}) collective-permute-start(f32[16,8,8,128]{3,0,2,1:T(8,128)S(1)} %get-tuple-element.15), channel_id=1, source_target_pairs={{0,64},{64,128},{128,192},{1,65},{65,129},{129,193},{2,66},{66,130... | collective-permute-start | bytes 1572872 | tf_op jit(solution)/shard_map/ppermute | solution.py:27
  683.5 22.1 %collective-permute-start.112 = (f32[16,8,8,128]{3,0,2,1:T(8,128)S(1)}, f32[16,8,8,128]{3,0,2,1:T(8,128)S(1)}, u32[]{:S(2)}, u32[]{:S(2)}) collective-permute-start(f32[16,8,8,128]{3,0,2,1:T(8,128)S(1)} %get-tuple-element.7), channel_id=1, source_target_pairs={{0,64},{64,128},{128,192},{1,65},{65,129},{129,193},{2,66},{66,130... | collective-permute-start | bytes 1572872 | tf_op jit(solution)/shard_map/ppermute | solution.py:27
  750.7 9.9 %collective-permute-start.123 = (f32[16,1,8,128]{3,0,2,1:T(8,128)S(1)}, f32[16,1,8,128]{3,0,2,1:T(8,128)S(1)}, u32[]{:S(2)}, u32[]{:S(2)}) collective-permute-start(f32[16,1,8,128]{3,0,2,1:T(8,128)S(1)} %get-tuple-element.144), channel_id=1, source_target_pairs={{4,0},{8,4},{12,8},{16,12},{20,16},{24,20},{28,24},{32,28},{36,32}... | collective-permute-start | bytes 196616 | tf_op jit(solution)/shard_map/ppermute | solution.py:19
  (152 other events, 2522.0 us)
where the time goes:
time: 785 us; the launch traced here: 773 us
  waiting for transfers between devices  383 us (49%)
  starting transfers between devices  329 us (42%)
  other arithmetic  40.7 us (5%)
  matrix products  12.6 us (2%)
    ppermute x56, waiting for transfers between devices, padded_2(): after = lax.ppermute(leading, axis, down)  258 us
    ppermute x56, starting transfers between devices, padded_2(): after = lax.ppermute(leading, axis, down)  148 us
    ppermute x56, starting transfers between devices, padded_2(): before = lax.ppermute(last, axis, up)  141 us
    ppermute x14, waiting for transfers between devices, from_behind(): lax.ppermute(value, axis, [(source, source + steps) for source in range(l...  125 us
    ppermute x14, starting transfers between devices, from_behind(): lax.ppermute(value, axis, [(source, source + steps) for source in range(l...  40.5 us
  transfers between devices with their start and end apart: 126, of which 69 were waited for; matrix products, arithmetic and copies ran while one was open for 2% of the time, Pallas kernels for 0%

commit v1 on v0

v1 whole, which is shorter than its diff:
```python
import functools

import jax
import jax.numpy as jnp
from jax import lax
from jax.experimental import pallas as pl
from jax.experimental.pallas import tpu as pltpu
from jax.sharding import PartitionSpec as P

MESH = pl.DeviceIdType.MESH
REACT = 11
STEPS = 4
LEVELS = 4
C = 16
NZ = 128
T = 4
W = 2
E = T + 2 * W
DIRS = ((1, 0), (-1, 0), (0, 1), (0, -1), (1, 1), (-1, -1), (1, -1), (-1, 1))


def spans(d):
    if d == 1:
        return W + T - W, 0, W
    if d == -1:
        return W, W + T, W
    return W, W, T


def corner_spans(d):
    return (W + T - 1, W - 1, 1) if d == 1 else (W, W + T, 1)


def box(dx, dy):
    if dx and dy:
        return corner_spans(dx), corner_spans(dy)
    return spans(dx), spans(dy)


def here():
    lvl, gx, gy = lax.axis_index("lvl"), lax.axis_index("gx"), lax.axis_index("gy")
    lx, ly = lvl // 2, (lvl + lvl // 2) % 2
    return 2 * gx + (lx + gx) % 2, 2 * gy + (ly + gy) % 2


def device_at(X, Y):
    gx, gy = X // 2, Y // 2
    lx, ly = (X % 2 + gx) % 2, (Y % 2 + gy) % 2
    return lx * (3 - 2 * ly) + ly, gx, gy


def kernel(nx, ny, ini, rf, dh_ref, lr_ref, wq_ref, wf_ref, out,
           stage, U, V2, V1, K, WX, WY, WZ, RHS, INV, ACC, INF, PQ, RF,
           i_send, i_recv, u_send, u_recv, v_send, v_recv, f_send, f_recv):
    lvl, gx, gy = lax.axis_index("lvl"), lax.axis_index("gx"), lax.axis_index("gy")
    X, Y = here()

    def exists(dx, dy):
        ok = None
        for d, at, n in ((dx, X, nx), (dy, Y, ny)):
            if d:
                c = at < n - 1 if d == 1 else at > 0
                ok = c if ok is None else ok & c
        return ok

    def each(f):
        for i, (dx, dy) in enumerate(DIRS):
            @pl.when(exists(dx, dy))
            def _():
                f(i, dx, dy)

    S0 = stage.at[1]
    zero = jnp.zeros((E, 24, NZ), jnp.float32)
    zero_v = jnp.zeros((E, C, NZ), jnp.float32)

    def clear(x, c):
        S0[x] = zero
        for p in range(LEVELS):
            V2[p, x] = zero_v
        return c

    lax.fori_loop(0, E, clear, 0)

    nat = stage.at[0]
    for x in range(8):
        nat[x, :, 0:C, :] = jnp.swapaxes(ini[:, x], 0, 1)
        nat[x, :, C:24, :] = jnp.broadcast_to(rf[x][:, None, :], (8, 8, NZ))

    bar = pltpu.get_barrier_semaphore()

    def greet(device):
        pl.semaphore_signal(bar, inc=1, device_id=device, device_id_type=MESH)

    each(lambda i, dx, dy: greet(device_at(X + dx, Y + dy)))
    for k in range(1, LEVELS):
        greet(((lvl + k) % LEVELS, gx, gy))
    beside = sum(exists(dx, dy).astype(jnp.int32) for dx, dy in DIRS)
    pl.semaphore_wait(bar, beside + LEVELS - 1)

    ox, oy = T * (X % 2), T * (Y % 2)

    def init_copy(i, dx, dy, device):
        (sx, tx, mx), (sy, ty, my) = box(dx, dy)
        return pltpu.make_async_remote_copy(
            src_ref=nat.at[pl.ds(ox + sx - W, mx), pl.ds(oy + sy - W, my)],
            dst_ref=S0.at[tx:tx + mx, ty:ty + my],
            send_sem=i_send.at[i], recv_sem=i_recv.at[i], device_id=device, device_id_type=MESH)

    each(lambda i, dx, dy: init_copy(i, dx, dy, device_at(X + dx, Y + dy)).start())
    for x in range(T):
        S0[W + x, W:W + T] = nat[ox + x, pl.ds(oy, T)]
    each(lambda i, dx, dy: init_copy(i ^ 1, -dx, -dy, device_at(X + dx, Y + dy)).wait_recv())
    for x in range(E):
        for h in range(2):
            RF[x, :, 8 * h:8 * h + 8, :] = S0[x, :, C:24, :]
    each(lambda i, dx, dy: init_copy(i, dx, dy, device_at(X + dx, Y + dy)).wait_send())

    def rim_copy(buf, send, recv, p, i, dx, dy, device):
        (sx, tx, mx), (sy, ty, my) = box(dx, dy)
        return pltpu.make_async_remote_copy(
            src_ref=buf.at[p, sx:sx + mx, sy:sy + my],
            dst_ref=buf.at[p, tx:tx + mx, ty:ty + my],
            send_sem=send.at[p, i], recv_sem=recv.at[p, i], device_id=device, device_id_type=MESH)

    def rim_start(buf, send, recv, p):
        each(lambda i, dx, dy: rim_copy(buf, send, recv, p, i, dx, dy, device_at(X + dx, Y + dy)).start())

    def rim_wait(buf, send, recv, p):
        each(lambda i, dx, dy: rim_copy(buf, send, recv, p, i ^ 1, -dx, -dy, device_at(X + dx, Y + dy)).wait_recv())
        each(lambda i, dx, dy: rim_copy(buf, send, recv, p, i, dx, dy, device_at(X + dx, Y + dy)).wait_send())

    def final_copy(p):
        return pltpu.make_async_remote_copy(
            src_ref=U.at[p, W:W + T, W:W + T],
            dst_ref=out.at[pl.ds(ox, T), pl.ds(oy, T)],
            send_sem=f_send.at[p], recv_sem=f_recv.at[lvl], device_id=(p, gx, gy), device_id_type=MESH)

    lane = lax.broadcasted_iota(jnp.int32, (1, C, NZ), 2)
    first, last = lane == 0, lane == NZ - 1
    R = [(W, W + T) if x in (W - 1, W + T) else (W - 1, W + T + 1) for x in range(E)]

    def up(v):
        return pltpu.roll(v, 1, 2)

    def down(v):
        return pltpu.roll(v, NZ - 1, 2)

    def sweep(p, src, dst, rows, cols):
        for x in rows:
            lo, hi = cols(x)
            for a in range(lo, hi, 2):
                b = min(a + 2, hi)
                c = src(x, a - 1, b + 1)
                v, wz = c[1:-1], WZ[p, x, a:b]
                wy = WY[p, x, a - 1:b]
                n = (WX[p, x - 1, a:b] * src(x - 1, a, b) + WX[p, x, a:b] * src(x + 1, a, b)
                     + wy[:-1] * c[:-2] + wy[1:] * c[2:] + wz * up(v) + down(wz * v))
                dst(x, a, b, (RHS[p, x, a:b] + n) * INV[p, x, a:b])

    def split(u):
        hi = u.astype(jnp.bfloat16)
        lo = (u - hi.astype(jnp.float32)).astype(jnp.bfloat16)
        return jnp.concatenate([hi, lo, hi], axis=0)

    def chemistry(p):
        def one(get, put):
            u = get().reshape(4 * C, NZ)
            for k, w_ref, v in ((0, wf_ref, u), (1, wq_ref, u * u)):
                put(k, jnp.dot(w_ref[...], split(v), preferred_element_type=jnp.float32).reshape(4, C, NZ))

        for x in range(W - 1, W + T + 1):
            def put(k, v, x=x):
                PQ[k, x, W:W + T] = v
            one(lambda: U[p, x, W:W + T], put)
        for y in (W - 1, W + T):
            def put(k, v, y=y):
                for x in range(T):
                    PQ[k, W + x, y] = v[x]
            one(lambda: U[p, W:W + T, y], put)

    def setup(p):
        dh = dh_ref[...][None]
        lr = lr_ref[...][None]
        for x in range(E):
            lo, hi = (W, W + T) if x in (0, E - 1) else (R[x] if x in (1, E - 2) else (0, E))
            if x in (1, E - 2):
                lo, hi = 1, E - 1
            for a in range(lo, hi, 2):
                u = U[p, x, a:a + 2]
                K[x, a:a + 2] = dh + dh * (u * u)
        chemistry(p)
        for x in range(W - 1, W + T + 1):
            lo, hi = R[x]
            for a in range(lo, hi, 2):
                b = a + 2
                kc = K[x, a - 1:b + 1]
                k = kc[1:-1]
                kw, ke = K[x - 1, a:b], K[x + 1, a:b]
                ww, we, ws, wn = k + kw, k + ke, k + kc[:-2], k + kc[2:]
                kl = jnp.where(first, dh, up(k))
                kh = jnp.where(last, dh, down(k))
                wl = k + kl
                total = ((ww + we) + (ws + wn)) + (wl + (k + kh))
                wz = jnp.where(first, 0.0, wl)
                if x <= W + T - 1:
                    WX[p, x - 1, a:b] = ww
                if x >= W + T - 1:
                    WX[p, x, a:b] = we
                WY[p, x, a - 1:b - 1] = ws
                if b == hi:
                    WY[p, x, b - 1:b] = wn[-1:]
                WZ[p, x, a:b] = wz
                uc = U[p, x, a - 1:b + 1]
                u = uc[1:-1]
                n = (ww * U[p, x - 1, a:b] + we * U[p, x + 1, a:b] + ws * uc[:-2] + wn * uc[2:]
                     + wz * up(u) + down(wz * u))
                r = RF[x, a:b]
                made = r * PQ[0, x, a:b]
                lost = total + r * (lr + PQ[1, x, a:b])
                half = 0.5 * ((n + made) - lost * u)
                inv = 1.0 / (1.0 + lost)
                inflow = INF[x, a:b]
                old = ACC[p, x, a:b]
                right = (u + made) + inflow
                INF[x, a:b] = (old + half) - u
                ACC[p, x, a:b] = (half + u) + inflow
                RHS[p, x, a:b] = right
                INV[p, x, a:b] = inv
                V1[x, a:b] = (right + n) * inv

    none_v = jnp.zeros((1, C, NZ), jnp.float32)

    def mask(p):
        for cond, cells in ((X == 0, [(W - 1, y) for y in range(W, W + T)]),
                            (X == nx - 1, [(W + T, y) for y in range(W, W + T)]),
                            (Y == 0, [(x, W - 1) for x in range(W, W + T)]),
                            (Y == ny - 1, [(x, W + T) for x in range(W, W + T)])):
            @pl.when(cond)
            def _():
                for x, y in cells:
                    V1[x, y:y + 1] = none_v
                    INV[p, x, y:y + 1] = none_v

    inner = range(W, W + T)
    outer = range(W - 1, W + T + 1)

    def store_v1(x, a, b, v):
        V1[x, a:b] = v

    def phase_a(t, p):
        n = t - p

        @pl.when((n >= 0) & ((n < STEPS) | ((n == STEPS) & (p < LEVELS - 1))))
        def _():
            @pl.when(n == 0)
            def _():
                for x in range(E):
                    U[p, x] = S0[x, :, 0:C, :]

            @pl.when(n > 0)
            def _():
                rim_wait(U, u_send, u_recv, p)

            setup(p)

            @pl.when(n < STEPS)
            def _():
                mask(p)

                def put(x, a, b, v):
                    V2[p, x, a:b] = v
                sweep(p, lambda x, a, b: V1[x, a:b], put, inner, lambda x: (W, W + T))
                rim_start(V2, v_send, v_recv, p)

    def phase_b(t, p):
        n = t - p

        @pl.when((n >= 0) & (n < STEPS))
        def _():
            rim_wait(V2, v_send, v_recv, p)
            sweep(p, lambda x, a, b: V2[p, x, a:b], store_v1, outer, lambda x: R[x])

            def put(x, a, b, v):
                U[p, x, a:b] = v
            sweep(p, lambda x, a, b: V1[x, a:b], put, inner, lambda x: (W, W + T))

            @pl.when((n < STEPS - 1) | (p < LEVELS - 1))
            def _():
                rim_start(U, u_send, u_recv, p)

            @pl.when(n == STEPS - 1)
            def _():
                @pl.when(p != lvl)
                def _():
                    final_copy(p).start()

                @pl.when(p == lvl)
                def _():
                    for x in range(T):
                        out[ox + x, pl.ds(oy, T)] = U[p, W + x, W:W + T]

    def tick(t, c):
        for x in range(1, E - 1):
            INF[x] = zero_v
        lax.fori_loop(0, LEVELS, lambda p, c: (phase_a(t, p), c)[1], 0)
        lax.fori_loop(0, LEVELS, lambda p, c: (phase_b(t, p), c)[1], 0)
        return c

    lax.fori_loop(0, STEPS + LEVELS - 1, tick, 0)

    for k in range(1, LEVELS):
        src = (lvl + k) % LEVELS
        pltpu.make_async_remote_copy(
            src_ref=U.at[0, W:W + T, W:W + T], dst_ref=out.at[0:T, 0:T],
            send_sem=f_send.at[0], recv_sem=f_recv.at[src], device_id=(src, gx, gy), device_id_type=MESH).wait_recv()
    for p in range(LEVELS):
        @pl.when(p != lvl)
        def _():
            final_copy(p).wait_send()


def on_device(nx, ny, initial, rate_factor, diffusivity, loss_rate, quench, formation):
    def rows(v):
        return jnp.broadcast_to(v[:, None], (C, NZ))

    reacting = jnp.arange(C) < REACT
    lr = jnp.where(reacting, loss_rate, 0.0)
    wide = jnp.eye(4, dtype=jnp.float32)

    def blocks(m):
        m = jnp.where(reacting[:, None], m, 0.0)
        big = (wide[:, None, :, None] * m[None, :, None, :]).reshape(4 * C, 4 * C)
        hi = lax.reduce_precision(big, 8, 7)
        lo = (big - hi).astype(jnp.bfloat16)
        hi = hi.astype(jnp.bfloat16)
        return jnp.concatenate([hi, hi, lo], axis=1)

    f32 = jnp.float32
    frame = (E, E, C, NZ)
    vmem = pl.BlockSpec(memory_space=pltpu.VMEM)
    dma = pltpu.SemaphoreType.DMA
    done = pl.pallas_call(
        functools.partial(kernel, nx, ny),
        name="deferred_correction",
        out_shape=jax.ShapeDtypeStruct((8, 8, C, NZ), f32),
        in_specs=[vmem] * 6,
        out_specs=vmem,
        scratch_shapes=[
            pltpu.VMEM((2, E, E, 24, NZ), f32),
            pltpu.VMEM((LEVELS,) + frame, f32),
            pltpu.VMEM((LEVELS,) + frame, f32),
            pltpu.VMEM(frame, f32),
            pltpu.VMEM(frame, f32),
            pltpu.VMEM((LEVELS,) + frame, f32),
            pltpu.VMEM((LEVELS,) + frame, f32),
            pltpu.VMEM((LEVELS,) + frame, f32),
            pltpu.VMEM((LEVELS,) + frame, f32),
            pltpu.VMEM((LEVELS,) + frame, f32),
            pltpu.VMEM((LEVELS,) + frame, f32),
            pltpu.VMEM(frame, f32),
            pltpu.VMEM((2,) + frame, f32),
            pltpu.VMEM(frame, f32),
            dma((8,)), dma((8,)),
            dma((LEVELS, 8)), dma((LEVELS, 8)),
            dma((LEVELS, 8)), dma((LEVELS, 8)),
            dma((LEVELS,)), dma((LEVELS,)),
        ],
        compiler_params=pltpu.CompilerParams(
            collective_id=0, has_side_effects=True, vmem_limit_bytes=44 << 20),
    )(initial, rate_factor, rows(0.5 * diffusivity), rows(lr), blocks(loss_rate[:, None] * quench), blocks(formation))
    return done.transpose(2, 0, 1, 3)[None]


def solution(mesh):
    in_specs = (P(None, "gx", "gy", None), P("gx", "gy", None), P(), P(), P(), P())
    out_specs = P("lvl", None, "gx", "gy", None)
    nx, ny = 2 * mesh.shape["gx"], 2 * mesh.shape["gy"]
    return jax.shard_map(
        functools.partial(on_device, nx, ny), mesh=mesh, in_specs=in_specs, out_specs=out_specs, check_vma=False)
```

time: 785 us -> 177 us (0.23)
  the two profiles are of different devices: /device:TPU:91 before, /device:TPU:94 now
where the time goes in v1:
time: 177 us; the launch traced here: 173 us
  Pallas kernels  170 us (96%)
  local copies, waits for them, and re-layouts  1.98 us (1%)
    pallas_call x1, Pallas kernels, on_device(): pl.pallas_call(functools.partial(kernel, nx, ny), name='deferred_correcti...  170 us

profile of v1, /device:TPU:94, one launch (start us, length us, event | category | flops | bytes accessed | tf_op | source)
XLA Modules:
  0.0 173.5 jit_solution(15795354455732377780)
XLA Ops:
  0.0 0.0 copy-start.2
  0.0 0.0 copy-start
  0.0 0.7 broadcast_multiply_fusion.2
  0.7 0.0 copy-done.2
  0.7 0.1 broadcast_in_dim.46.lr_ref
  0.8 0.1 broadcast_in_dim.44.dh_ref
  0.9 0.8 broadcast_select_fusion
  1.7 0.1 broadcast_multiply_fusion
  1.8 0.1 mul.54
  1.9 0.1 mul.51
  2.1 0.0 copy-start.1
  2.1 0.1 pad_maximum_fusion
  2.2 0.0 copy-done
  2.2 0.6 copy-done.1
  2.8 169.7 %deferred_correction.1 = f32[8,8,16,128]{3,2,1,0:T(8,128)S(1)} custom-call(f32[16,8,8,128]{3,2,1,0:T(8,128)S(1)} %copy-done, f32[8,8,128]{2,1,0:T(8,128)S(1)} %copy-done.1, f32[16,128]{1,0:T(8,128)S(1)} %broadcast_in_dim.44.dh_ref, f32[16,128]{1,0:T(8,128)S(1)} %broadcast_in_dim.46.lr_ref, bf16[64,192]{1,0:T(8,128)(2,1)S(1)} %get-tuple-element.13.wq_ref, ...), custom_call_target="tpu_custom_call" | custom-call | tf_op jit(solution)/shard_map/deferred_correction/pallas_call | solution.py:342
  172.5 1.0 copy.7
  (5 shorter events, 0.0 us)
Async XLA Ops:
  0.0 0.7 copy-start.2
  0.0 2.2 %copy-start = (f32[16,8,8,128]{3,2,1,0:T(8,128)S(1)}, f32[16,8,8,128]{3,2,1,0:T(8,128)}, u32[]{:S(2)}) copy-start(f32[16,8,8,128]{3,2,1,0:T(8,128)} %ini.1) | copy-start | bytes 1572868
  2.1 0.8 copy-start.1

commit v2 on v1

--- a/solution.py
+++ b/solution.py
@@ -39,21 +39,31 @@
 
 def here():
     lvl, gx, gy = lax.axis_index("lvl"), lax.axis_index("gx"), lax.axis_index("gy")
-    lx, ly = lvl // 2, (lvl + lvl // 2) % 2
-    return 2 * gx + (lx + gx) % 2, 2 * gy + (ly + gy) % 2
+    y = gx % 4
+    back = y // 2
+    m = (y + back) % 2
+    strip = 4 * (gx // 4) + m + (gy // 2) * (3 - 2 * m)
+    return 2 * strip + gy % 2, lvl + back * (7 - 2 * lvl)
 
 
 def device_at(X, Y):
-    gx, gy = X // 2, Y // 2
-    lx, ly = (X % 2 + gx) % 2, (Y % 2 + gy) % 2
-    return lx * (3 - 2 * ly) + ly, gx, gy
-
-
-def kernel(nx, ny, ini, rf, dh_ref, lr_ref, wq_ref, wf_ref, out,
-           stage, U, V2, V1, K, WX, WY, WZ, RHS, INV, ACC, INF, PQ, RF,
-           i_send, i_recv, u_send, u_recv, v_send, v_recv, f_send, f_recv):
+    strip, back, r = X // 2, Y // 4, Y % 4
+    s = strip % 4
+    m = (s + s // 2) % 2
+    y = m + back * (3 - 2 * m)
+    return r + back * (3 - 2 * r), 4 * (strip // 4) + y, 2 * (s // 2) + X % 2
+
+
+def kernel(nx, ny, ini, rf, d_ref, l_ref, quench_ref, formation_ref, out,
+           stage, U, V2, V1, K, WX, WY, WZ, RHS, INV, ACC, INF, PQ, RF, flat, flat24,
+           dh_ref, lr_ref, wq_ref, wf_ref, G,
+           i_send, i_recv, u_send, u_recv, v_send, v_recv, g_send, g_recv, f_send, f_recv):
     lvl, gx, gy = lax.axis_index("lvl"), lax.axis_index("gx"), lax.axis_index("gy")
+    me = (lvl, gx, gy)
     X, Y = here()
+
+    def other(device):
+        return (device[0] != lvl) | (device[1] != gx) | (device[2] != gy)
 
     def exists(dx, dy):
         ok = None
@@ -63,15 +73,24 @@
                 ok = c if ok is None else ok & c
         return ok
 
+    beside = [(exists(dx, dy), device_at(X + dx, Y + dy)) for dx, dy in DIRS]
+    gives = lvl // 2 == (gy + gy // 2) % 2
+    YA = lvl + (gy // 2) * (7 - 2 * lvl)
+    takers = [device_at(2 * gx + e, YA) for e in range(2)]
+    giver = (lvl, X // 2, Y // 2)
+    row_of_four = [((lvl + k) % LEVELS, gx, gy) for k in range(1, LEVELS)]
+
     def each(f):
         for i, (dx, dy) in enumerate(DIRS):
-            @pl.when(exists(dx, dy))
-            def _():
-                f(i, dx, dy)
+            @pl.when(beside[i][0])
+            def _():
+                f(i, dx, dy, beside[i][1])
 
     S0 = stage.at[1]
     zero = jnp.zeros((E, 24, NZ), jnp.float32)
     zero_v = jnp.zeros((E, C, NZ), jnp.float32)
+
+    edge_x, edge_y = (X == 0) | (X == nx - 1), (Y == 0) | (Y == ny - 1)
 
     def clear(x, c):
         S0[x] = zero
@@ -79,61 +98,128 @@
             V2[p, x] = zero_v
         return c
 
-    lax.fori_loop(0, E, clear, 0)
+    @pl.when(edge_x | edge_y)
+    def _():
+        lax.fori_loop(0, E, clear, 0)
+
+    bar = pltpu.get_barrier_semaphore()
+
+    def greet(device):
+        pl.semaphore_signal(bar, inc=1, device_id=device, device_id_type=MESH)
+
+    each(lambda i, dx, dy, device: greet(device))
+    others = [(lvl >= 0, device) for device in row_of_four]
+    others += [(gives & other(device), device) for device in takers] + [(other(giver), giver)]
+    for cond, device in others:
+        @pl.when(cond)
+        def _():
+            greet(device)
+
+    reacts = lax.broadcasted_iota(jnp.int32, (C, NZ), 0) < REACT
+    dh_ref[...] = jnp.broadcast_to(0.5 * d_ref[...], (C, NZ))
+    lr_ref[...] = jnp.where(reacts, jnp.broadcast_to(l_ref[...], (C, NZ)), 0.0)
+    row, col = (lax.broadcasted_iota(jnp.int32, (4 * C, 4 * C), k) for k in range(2))
+    for w_ref, m in ((wq_ref, quench_ref[...] * l_ref[...]), (wf_ref, formation_ref[...])):
+        m = jnp.concatenate([jnp.concatenate([m] * 4, axis=1)] * 4, axis=0)
+        m = jnp.where((row // C == col // C) & (row % C < REACT), m, 0.0)
+        hi = m.astype(jnp.bfloat16).astype(jnp.float32)
+        w_ref[...] = jnp.concatenate([hi, hi, m - hi], axis=1).astype(jnp.bfloat16)
 
     nat = stage.at[0]
     for x in range(8):
         nat[x, :, 0:C, :] = jnp.swapaxes(ini[:, x], 0, 1)
         nat[x, :, C:24, :] = jnp.broadcast_to(rf[x][:, None, :], (8, 8, NZ))
 
-    bar = pltpu.get_barrier_semaphore()
-
-    def greet(device):
-        pl.semaphore_signal(bar, inc=1, device_id=device, device_id_type=MESH)
-
-    each(lambda i, dx, dy: greet(device_at(X + dx, Y + dy)))
-    for k in range(1, LEVELS):
-        greet(((lvl + k) % LEVELS, gx, gy))
-    beside = sum(exists(dx, dy).astype(jnp.int32) for dx, dy in DIRS)
-    pl.semaphore_wait(bar, beside + LEVELS - 1)
-
-    ox, oy = T * (X % 2), T * (Y % 2)
-
-    def init_copy(i, dx, dy, device):
+    count = sum(ok.astype(jnp.int32) for ok, _ in beside) + sum(cond.astype(jnp.int32) for cond, _ in others)
+    pl.semaphore_wait(bar, count)
+
+    def hand(e, device):
+        return pltpu.make_async_remote_copy(
+            src_ref=nat.at[T * e:T * e + T, pl.ds(T * (YA % 2), T)],
+            dst_ref=S0.at[W:W + T, W:W + T],
+            send_sem=i_send.at[1 + e], recv_sem=i_recv.at[1], device_id=device, device_id_type=MESH)
+
+    for e, device in enumerate(takers):
+        @pl.when(gives & other(device))
+        def _():
+            hand(e, device).start()
+
+        @pl.when(gives & jnp.logical_not(other(device)))
+        def _():
+            for x in range(T):
+                S0[W + x, W:W + T] = nat[T * e + x, pl.ds(T * (YA % 2), T)]
+
+    @pl.when(other(giver))
+    def _():
+        hand(0, giver).wait_recv()
+
+    def rim_copy(ref, send, recv, dx, dy, device):
         (sx, tx, mx), (sy, ty, my) = box(dx, dy)
         return pltpu.make_async_remote_copy(
-            src_ref=nat.at[pl.ds(ox + sx - W, mx), pl.ds(oy + sy - W, my)],
-            dst_ref=S0.at[tx:tx + mx, ty:ty + my],
-            send_sem=i_send.at[i], recv_sem=i_recv.at[i], device_id=device, device_id_type=MESH)
-
-    each(lambda i, dx, dy: init_copy(i, dx, dy, device_at(X + dx, Y + dy)).start())
-    for x in range(T):
-        S0[W + x, W:W + T] = nat[ox + x, pl.ds(oy, T)]
-    each(lambda i, dx, dy: init_copy(i ^ 1, -dx, -dy, device_at(X + dx, Y + dy)).wait_recv())
+            src_ref=ref.at[sx:sx + mx, sy:sy + my], dst_ref=ref.at[tx:tx + mx, ty:ty + my],
+            send_sem=send, recv_sem=recv, device_id=device, device_id_type=MESH)
+
+    inside = jnp.logical_not(edge_x | edge_y)
+    at_corner = edge_x & edge_y
+    at_edge = (edge_x | edge_y) & jnp.logical_not(at_corner)
+
+    def rim_wait_for(ref, send, recv):
+        for cond, cells in ((inside, 8 * W + 8 * W + 4), (at_edge, 12 * W + 2), (at_corner, 8 * W + 1)):
+            @pl.when(cond)
+            def _():
+                copy = pltpu.make_async_remote_copy(
+                    src_ref=ref.at[0:cells], dst_ref=ref.at[0:cells],
+                    send_sem=send, recv_sem=recv, device_id=me, device_id_type=MESH)
+                copy.wait_recv()
+                copy.wait_send()
+
+    each(lambda i, dx, dy, device: rim_copy(S0, i_send.at[0], i_recv.at[0], dx, dy, device).start())
+    rim_wait_for(flat24, i_send.at[0], i_recv.at[0])
     for x in range(E):
         for h in range(2):
             RF[x, :, 8 * h:8 * h + 8, :] = S0[x, :, C:24, :]
-    each(lambda i, dx, dy: init_copy(i, dx, dy, device_at(X + dx, Y + dy)).wait_send())
-
-    def rim_copy(buf, send, recv, p, i, dx, dy, device):
-        (sx, tx, mx), (sy, ty, my) = box(dx, dy)
+
+    def rim_start(buf, send, recv, p):
+        each(lambda i, dx, dy, device: rim_copy(buf.at[p], send.at[p], recv.at[p], dx, dy, device).start())
+
+    def rim_wait(buf, send, recv, p):
+        rim_wait_for(flat, send.at[p], recv.at[p])
+
+    def back_copy(p, e, device):
         return pltpu.make_async_remote_copy(
-            src_ref=buf.at[p, sx:sx + mx, sy:sy + my],
-            dst_ref=buf.at[p, tx:tx + mx, ty:ty + my],
-            send_sem=send.at[p, i], recv_sem=recv.at[p, i], device_id=device, device_id_type=MESH)
-
-    def rim_start(buf, send, recv, p):
-        each(lambda i, dx, dy: rim_copy(buf, send, recv, p, i, dx, dy, device_at(X + dx, Y + dy)).start())
-
-    def rim_wait(buf, send, recv, p):
-        each(lambda i, dx, dy: rim_copy(buf, send, recv, p, i ^ 1, -dx, -dy, device_at(X + dx, Y + dy)).wait_recv())
-        each(lambda i, dx, dy: rim_copy(buf, send, recv, p, i, dx, dy, device_at(X + dx, Y + dy)).wait_send())
-
-    def final_copy(p):
+            src_ref=U.at[p, W:W + T, W:W + T], dst_ref=G.at[p, pl.ds(T * e, T)],
+            send_sem=g_send.at[p], recv_sem=g_recv.at[p, e], device_id=device, device_id_type=MESH)
+
+    def back_start(p):
+        @pl.when(other(giver))
+        def _():
+            back_copy(p, X % 2, giver).start()
+
+        @pl.when(jnp.logical_not(other(giver)))
+        def _():
+            for x in range(T):
+                G[p, T * (X % 2) + x] = U[p, W + x, W:W + T]
+
+    def along_copy(p, e, source, YS):
         return pltpu.make_async_remote_copy(
-            src_ref=U.at[p, W:W + T, W:W + T],
-            dst_ref=out.at[pl.ds(ox, T), pl.ds(oy, T)],
-            send_sem=f_send.at[p], recv_sem=f_recv.at[lvl], device_id=(p, gx, gy), device_id_type=MESH)
+            src_ref=G.at[p, T * e:T * e + T], dst_ref=out.at[T * e:T * e + T, pl.ds(T * (YS % 2), T)],
+            send_sem=f_send.at[p, e], recv_sem=f_recv.at[source % 2, e], device_id=(p, gx, gy), device_id_type=MESH)
+
+    def along_start(p, e):
+        @pl.when(gives)
+        def _():
+            @pl.when(other(takers[e]))
+            def _():
+                back_copy(p, e, takers[e]).wait_recv()
+
+            @pl.when(p != lvl)
+            def _():
+                along_copy(p, e, lvl, YA).start()
+
+            @pl.when(p == lvl)
+            def _():
+                for x in range(T):
+                    out[T * e + x, pl.ds(T * (YA % 2), T)] = G[p, T * e + x]
 
     lane = lax.broadcasted_iota(jnp.int32, (1, C, NZ), 2)
     first, last = lane == 0, lane == NZ - 1
@@ -290,51 +376,55 @@
 
             @pl.when(n == STEPS - 1)
             def _():
-                @pl.when(p != lvl)
-                def _():
-                    final_copy(p).start()
-
-                @pl.when(p == lvl)
-                def _():
-                    for x in range(T):
-                        out[ox + x, pl.ds(oy, T)] = U[p, W + x, W:W + T]
+                back_start(p)
 
     def tick(t, c):
         for x in range(1, E - 1):
             INF[x] = zero_v
         lax.fori_loop(0, LEVELS, lambda p, c: (phase_a(t, p), c)[1], 0)
+
+        @pl.when(t >= LEVELS)
+        def _():
+            along_start(t - LEVELS, 0)
+
         lax.fori_loop(0, LEVELS, lambda p, c: (phase_b(t, p), c)[1], 0)
+
+        @pl.when(t >= LEVELS)
+        def _():
+            along_start(t - LEVELS, 1)
+
         return c
 
     lax.fori_loop(0, STEPS + LEVELS - 1, tick, 0)
 
-    for k in range(1, LEVELS):
-        src = (lvl + k) % LEVELS
-        pltpu.make_async_remote_copy(
-            src_ref=U.at[0, W:W + T, W:W + T], dst_ref=out.at[0:T, 0:T],
-            send_sem=f_send.at[0], recv_sem=f_recv.at[src], device_id=(src, gx, gy), device_id_type=MESH).wait_recv()
+    for e in range(2):
+        along_start(LEVELS - 1, e)
+
+    first_source = 2 * ((gy + gy // 2) % 2)
+    for k in range(2):
+        source = first_source + k
+
+        @pl.when(source != lvl)
+        def _():
+            for e in range(2):
+                along_copy(lvl, e, source, source + (gy // 2) * (7 - 2 * source)).wait_recv()
     for p in range(LEVELS):
-        @pl.when(p != lvl)
-        def _():
-            final_copy(p).wait_send()
+        @pl.when(other(giver))
+        def _():
+            back_copy(p, X % 2, giver).wait_send()
+
+        @pl.when(gives & (p != lvl))
+        def _():
+            for e in range(2):
+                along_copy(p, e, lvl, YA).wait_send()
+
+    for e, device in enumerate(takers):
+        @pl.when(gives & other(device))
+        def _():
+            hand(e, device).wait_send()
 
 
 def on_device(nx, ny, initial, rate_factor, diffusivity, loss_rate, quench, formation):
-    def rows(v):
-        return jnp.broadcast_to(v[:, None], (C, NZ))
-
-    reacting = jnp.arange(C) < REACT
-    lr = jnp.where(reacting, loss_rate, 0.0)
-    wide = jnp.eye(4, dtype=jnp.float32)
-
-    def blocks(m):
-        m = jnp.where(reacting[:, None], m, 0.0)
-        big = (wide[:, None, :, None] * m[None, :, None, :]).reshape(4 * C, 4 * C)
-        hi = lax.reduce_precision(big, 8, 7)
-        lo = (big - hi).astype(jnp.bfloat16)
-        hi = hi.astype(jnp.bfloat16)
-        return jnp.concatenate([hi, hi, lo], axis=1)
-
     f32 = jnp.float32
     frame = (E, E, C, NZ)
     vmem = pl.BlockSpec(memory_space=pltpu.VMEM)
@@ -360,14 +450,20 @@
             pltpu.VMEM(frame, f32),
             pltpu.VMEM((2,) + frame, f32),
             pltpu.VMEM(frame, f32),
-            dma((8,)), dma((8,)),
-            dma((LEVELS, 8)), dma((LEVELS, 8)),
-            dma((LEVELS, 8)), dma((LEVELS, 8)),
+            pltpu.VMEM((16 * W + 4, C, NZ), f32),
+            pltpu.VMEM((16 * W + 4, 24, NZ), f32),
+            pltpu.VMEM((C, NZ), f32), pltpu.VMEM((C, NZ), f32),
+            pltpu.VMEM((4 * C, 12 * C), jnp.bfloat16), pltpu.VMEM((4 * C, 12 * C), jnp.bfloat16),
+            pltpu.VMEM((LEVELS, 2 * T, T, C, NZ), f32),
+            dma((3,)), dma((2,)),
             dma((LEVELS,)), dma((LEVELS,)),
+            dma((LEVELS,)), dma((LEVELS,)),
+            dma((LEVELS,)), dma((LEVELS, 2)),
+            dma((LEVELS, 2)), dma((2, 2)),
         ],
         compiler_params=pltpu.CompilerParams(
             collective_id=0, has_side_effects=True, vmem_limit_bytes=44 << 20),
-    )(initial, rate_factor, rows(0.5 * diffusivity), rows(lr), blocks(loss_rate[:, None] * quench), blocks(formation))
+    )(initial, rate_factor, diffusivity[:, None], loss_rate[:, None], quench, formation)
     return done.transpose(2, 0, 1, 3)[None]
 
 

time: 177 us -> 118 us (0.67); the launches traced: 173 us -> 117 us
  Pallas kernels: 170 us -> 113 us
  local copies, waits for them, and re-layouts: 1.98 us -> 4.12 us
    pallas_call x1, Pallas kernels: 170 us -> 113 us  [on_device(): pl.pallas_call(functools.partial(kernel, nx, ny), name='deferred_correcti...]
    unnamed x6 -> x12, local copies, waits for them, and re-layouts: 0.65 us -> 3 us
where the time goes in v2:
time: 118 us; the launch traced here: 117 us
  Pallas kernels  113 us (96%)
  local copies, waits for them, and re-layouts  4.12 us (3%)
    pallas_call x1, Pallas kernels, on_device(): pl.pallas_call(functools.partial(kernel, nx, ny), name='deferred_correcti...  113 us
    unnamed x12, local copies, waits for them, and re-layouts  3 us

profile of v2, /device:TPU:94, one launch (start us, length us, event | category | flops | bytes accessed | tf_op | source)
XLA Modules:
  0.0 117.4 jit_solution(20164760184982917)
XLA Ops:
  0.0 0.0 copy-start.4
  0.0 0.0 copy-start.5
  0.0 0.7 copy-done.4
  0.7 0.0 copy-start.2
  0.7 0.0 copy-start.3
  0.7 0.1 copy.7.d_ref
  0.7 0.0 copy-done.5
  0.7 0.1 copy.8.l_ref
  0.8 0.5 copy-done.2
  1.4 0.0 copy-done.3
  1.4 0.0 copy-start
  1.4 1.0 copy-done
  2.4 0.0 copy-start.1
  2.4 0.8 copy-done.1
  3.2 113.2 %deferred_correction.1 = f32[8,8,16,128]{3,2,1,0:T(8,128)S(1)} custom-call(f32[16,8,8,128]{3,2,1,0:T(8,128)S(1)} %copy-done, f32[8,8,128]{2,1,0:T(8,128)S(1)} %copy-done.1, f32[16,1]{1,0:T(8,128)S(1)} %copy.7.d_ref, f32[16,1]{1,0:T(8,128)S(1)} %copy.8.l_ref, f32[16,16]{1,0:T(8,128)S(1)} %copy-done.2, f32[16,16]{1,0:T(8,128)S(1)} %copy-done.3), custom_call_target="tpu_custom_call" | custom-call | tf_op jit(solution)/shard_map/deferred_correction/pallas_call | solution.py:432
  116.4 1.0 copy.9
Async XLA Ops:
  0.0 0.7 copy-start.4
  0.0 0.7 copy-start.5
  0.7 0.7 copy-start.2
  0.7 0.7 copy-start.3
  1.4 1.0 copy-start
  2.4 0.8 copy-start.1

commit v3 on v2

--- a/solution.py
+++ b/solution.py
@@ -16,7 +16,7 @@
 T = 4
 W = 2
 E = T + 2 * W
-DIRS = ((1, 0), (-1, 0), (0, 1), (0, -1), (1, 1), (-1, -1), (1, -1), (-1, 1))
+DIRS = ((1, 1), (-1, -1), (1, -1), (-1, 1), (0, 1), (0, -1), (1, 0), (-1, 0))
 
 
 def spans(d):

time: 118 us -> 114 us (0.966)
  Pallas kernels: 113 us -> 109 us
    pallas_call x1, Pallas kernels: 113 us -> 109 us  [on_device(): pl.pallas_call(functools.partial(kernel, nx, ny), name='deferred_correcti...]
where the time goes in v3:
time: 114 us
  Pallas kernels  109 us (96%)
  local copies, waits for them, and re-layouts  4.12 us (4%)
    pallas_call x1, Pallas kernels, on_device(): pl.pallas_call(functools.partial(kernel, nx, ny), name='deferred_correcti...  109 us
    unnamed x12, local copies, waits for them, and re-layouts  3 us

profile of v3, /device:TPU:94, one launch (start us, length us, event | category | flops | bytes accessed | tf_op | source)
XLA Modules:
  0.0 113.6 jit_solution(7025595733640416742)
XLA Ops:
  0.0 0.0 copy-start.4
  0.0 0.0 copy-start.5
  0.0 0.7 copy-done.4
  0.7 0.0 copy-start.2
  0.7 0.0 copy-start.3
  0.7 0.1 copy.7.d_ref
  0.7 0.0 copy-done.5
  0.7 0.1 copy.8.l_ref
  0.8 0.5 copy-done.2
  1.4 0.0 copy-done.3
  1.4 0.0 copy-start
  1.4 1.0 copy-done
  2.4 0.0 copy-start.1
  2.4 0.8 copy-done.1
  3.2 109.5 %deferred_correction.1 = f32[8,8,16,128]{3,2,1,0:T(8,128)S(1)} custom-call(f32[16,8,8,128]{3,2,1,0:T(8,128)S(1)} %copy-done, f32[8,8,128]{2,1,0:T(8,128)S(1)} %copy-done.1, f32[16,1]{1,0:T(8,128)S(1)} %copy.7.d_ref, f32[16,1]{1,0:T(8,128)S(1)} %copy.8.l_ref, f32[16,16]{1,0:T(8,128)S(1)} %copy-done.2, f32[16,16]{1,0:T(8,128)S(1)} %copy-done.3), custom_call_target="tpu_custom_call" | custom-call | tf_op jit(solution)/shard_map/deferred_correction/pallas_call | solution.py:432
  112.6 1.0 copy.9
Async XLA Ops:
  0.0 0.7 copy-start.4
  0.0 0.7 copy-start.5
  0.7 0.7 copy-start.2
  0.7 0.7 copy-start.3
  1.4 1.0 copy-start
  2.4 0.8 copy-start.1

commit v4 on v3

--- a/solution.py
+++ b/solution.py
@@ -277,8 +277,8 @@
         chemistry(p)
         for x in range(W - 1, W + T + 1):
             lo, hi = R[x]
-            for a in range(lo, hi, 2):
-                b = a + 2
+            for a in range(lo, hi, hi - lo):
+                b = hi
                 kc = K[x, a - 1:b + 1]
                 k = kc[1:-1]
                 kw, ke = K[x - 1, a:b], K[x + 1, a:b]

time: 114 us -> 112 us (0.982)
  Pallas kernels: 109 us -> 107 us
    pallas_call x1, Pallas kernels: 109 us -> 107 us  [on_device(): pl.pallas_call(functools.partial(kernel, nx, ny), name='deferred_correcti...]
where the time goes in v4:
time: 112 us
  Pallas kernels  107 us (96%)
  local copies, waits for them, and re-layouts  4.12 us (4%)
    pallas_call x1, Pallas kernels, on_device(): pl.pallas_call(functools.partial(kernel, nx, ny), name='deferred_correcti...  107 us
    unnamed x12, local copies, waits for them, and re-layouts  3 us

profile of v4, /device:TPU:94, one launch (start us, length us, event | category | flops | bytes accessed | tf_op | source)
XLA Modules:
  0.0 111.6 jit_solution(17685289114164267609)
XLA Ops:
  0.0 0.0 copy-start.4
  0.0 0.0 copy-start.5
  0.0 0.7 copy-done.4
  0.7 0.0 copy-start.2
  0.7 0.0 copy-start.3
  0.7 0.1 copy.7.d_ref
  0.7 0.0 copy-done.5
  0.7 0.1 copy.8.l_ref
  0.8 0.5 copy-done.2
  1.4 0.0 copy-done.3
  1.4 0.0 copy-start
  1.4 1.0 copy-done
  2.4 0.0 copy-start.1
  2.4 0.8 copy-done.1
  3.2 107.5 %deferred_correction.1 = f32[8,8,16,128]{3,2,1,0:T(8,128)S(1)} custom-call(f32[16,8,8,128]{3,2,1,0:T(8,128)S(1)} %copy-done, f32[8,8,128]{2,1,0:T(8,128)S(1)} %copy-done.1, f32[16,1]{1,0:T(8,128)S(1)} %copy.7.d_ref, f32[16,1]{1,0:T(8,128)S(1)} %copy.8.l_ref, f32[16,16]{1,0:T(8,128)S(1)} %copy-done.2, f32[16,16]{1,0:T(8,128)S(1)} %copy-done.3), custom_call_target="tpu_custom_call" | custom-call | tf_op jit(solution)/shard_map/deferred_correction/pallas_call | solution.py:432
  110.7 1.0 copy.9
Async XLA Ops:
  0.0 0.7 copy-start.4
  0.0 0.7 copy-start.5
  0.7 0.7 copy-start.2
  0.7 0.7 copy-start.3
  1.4 1.0 copy-start
  2.4 0.8 copy-start.1

commit v5 on v4

--- a/solution.py
+++ b/solution.py
@@ -248,17 +248,17 @@
         lo = (u - hi.astype(jnp.float32)).astype(jnp.bfloat16)
         return jnp.concatenate([hi, lo, hi], axis=0)
 
-    def chemistry(p):
+    def chemistry(p, own):
         def one(get, put):
             u = get().reshape(4 * C, NZ)
             for k, w_ref, v in ((0, wf_ref, u), (1, wq_ref, u * u)):
                 put(k, jnp.dot(w_ref[...], split(v), preferred_element_type=jnp.float32).reshape(4, C, NZ))
 
-        for x in range(W - 1, W + T + 1):
+        for x in range(W, W + T) if own else (W - 1, W + T):
             def put(k, v, x=x):
                 PQ[k, x, W:W + T] = v
             one(lambda: U[p, x, W:W + T], put)
-        for y in (W - 1, W + T):
+        for y in () if own else (W - 1, W + T):
             def put(k, v, y=y):
                 for x in range(T):
                     PQ[k, W + x, y] = v[x]
@@ -274,7 +274,7 @@
             for a in range(lo, hi, 2):
                 u = U[p, x, a:a + 2]
                 K[x, a:a + 2] = dh + dh * (u * u)
-        chemistry(p)
+        chemistry(p, False)
         for x in range(W - 1, W + T + 1):
             lo, hi = R[x]
             for a in range(lo, hi, hi - lo):
@@ -343,6 +343,8 @@
                 for x in range(E):
                     U[p, x] = S0[x, :, 0:C, :]
 
+            chemistry(p, True)
+
             @pl.when(n > 0)
             def _():
                 rim_wait(U, u_send, u_recv, p)

time: 112 us -> 112 us (level)
  no operation moved by 1% of the time
where the time goes in v5:
time: 112 us
  Pallas kernels  108 us (96%)
  local copies, waits for them, and re-layouts  4.12 us (4%)
    pallas_call x1, Pallas kernels, on_device(): pl.pallas_call(functools.partial(kernel, nx, ny), name='deferred_correcti...  108 us
    unnamed x12, local copies, waits for them, and re-layouts  3 us

profile of v5, /device:TPU:94, one launch (start us, length us, event | category | flops | bytes accessed | tf_op | source)
XLA Modules:
  0.0 111.9 jit_solution(1335181017072509344)
XLA Ops:
  0.0 0.0 copy-start.4
  0.0 0.0 copy-start.5
  0.0 0.7 copy-done.4
  0.7 0.0 copy-start.2
  0.7 0.0 copy-start.3
  0.7 0.1 copy.7.d_ref
  0.7 0.0 copy-done.5
  0.7 0.1 copy.8.l_ref
  0.8 0.5 copy-done.2
  1.4 0.0 copy-done.3
  1.4 0.0 copy-start
  1.4 1.0 copy-done
  2.4 0.0 copy-start.1
  2.4 0.8 copy-done.1
  3.2 107.7 %deferred_correction.1 = f32[8,8,16,128]{3,2,1,0:T(8,128)S(1)} custom-call(f32[16,8,8,128]{3,2,1,0:T(8,128)S(1)} %copy-done, f32[8,8,128]{2,1,0:T(8,128)S(1)} %copy-done.1, f32[16,1]{1,0:T(8,128)S(1)} %copy.7.d_ref, f32[16,1]{1,0:T(8,128)S(1)} %copy.8.l_ref, f32[16,16]{1,0:T(8,128)S(1)} %copy-done.2, f32[16,16]{1,0:T(8,128)S(1)} %copy-done.3), custom_call_target="tpu_custom_call" | custom-call | tf_op jit(solution)/shard_map/deferred_correction/pallas_call | solution.py:434
  110.9 1.0 copy.9
Async XLA Ops:
  0.0 0.7 copy-start.4
  0.0 0.7 copy-start.5
  0.7 0.7 copy-start.2
  0.7 0.7 copy-start.3
  1.4 1.0 copy-start
  2.4 0.8 copy-start.1
